TPU v7x, 32 devices: a whole 2x2x4 slice. The times are simulated.
32 devices in a mesh: seq: 8 (over y, x, core), head: 4 (over z).
Axes of the slice: x: 2, y: 2, z: 4, core: 2. Of those that a mesh axis runs over, the one named last changes fastest.
Arguments:
- hidden_in: float32 [4096, 768], P('seq'), may hold values from -6 to 6
- grad_out: float32 [4096, 768], P('seq'), may hold values from -6 to 6
- doc_lengths: int32 [3], replicated, may hold values from 1 to 2048, as said below
- norm_gain: float32 [2, 768], replicated, may hold values from 0.5 to 1.5
- proj_z: float32 [2, 768, 1536], P(None, 'seq', 'head'), may hold values from -0.21875 to 0.21875
- proj_x: float32 [2, 768, 1536], P(None, 'seq', 'head'), may hold values from -0.21875 to 0.21875
- proj_bc: float32 [2, 768, 256], P(None, 'seq', 'head'), may hold values from -0.21875 to 0.21875
- proj_dt: float32 [2, 768, 24], P(None, 'seq', 'head'), may hold values from -0.21875 to 0.21875
- conv_x_kernel: float32 [2, 4, 1536], P(None, None, 'head'), may hold values from -3 to 3
- conv_x_bias: float32 [2, 1536], P(None, 'head'), may hold values from -0.5 to 0.5
- conv_bc_kernel: float32 [2, 4, 256], P(None, None, 'head'), may hold values from -3 to 3
- conv_bc_bias: float32 [2, 256], P(None, 'head'), may hold values from -0.5 to 0.5
- dt_bias: float32 [2, 24], P(None, 'head'), may hold values from -6 to -3
- a_log: float32 [2, 24], P(None, 'head'), may hold values from -3 to 2
- skip_gain: float32 [2, 24], P(None, 'head'), may hold values from 0.5 to 1.5
- gate_gain: float32 [2, 1536], P(None, 'head'), may hold values from 0.5 to 1.5
- proj_out: float32 [2, 768, 1536], P(None, 'seq', 'head'), may hold values from -0.15625 to 0.15625
Outputs:
- hidden_out: float32 [4096, 768], P('seq')
- grad_hidden: float32 [4096, 768], P('seq')
- grad_norm_gain: float32 [2, 768], replicated
- grad_proj_z: float32 [2, 768, 1536], P(None, 'seq', 'head')
- grad_proj_x: float32 [2, 768, 1536], P(None, 'seq', 'head')
- grad_proj_bc: float32 [2, 768, 256], P(None, 'seq', 'head')
- grad_proj_dt: float32 [2, 768, 24], P(None, 'seq', 'head')
- grad_conv_x_kernel: float32 [2, 4, 1536], P(None, None, 'head')
- grad_conv_x_bias: float32 [2, 1536], P(None, 'head')
- grad_conv_bc_kernel: float32 [2, 4, 256], P(None, None, 'head')
- grad_conv_bc_bias: float32 [2, 256], P(None, 'head')
- grad_dt_bias: float32 [2, 24], P(None, 'head')
- grad_a_log: float32 [2, 24], P(None, 'head')
- grad_skip_gain: float32 [2, 24], P(None, 'head')
- grad_gate_gain: float32 [2, 1536], P(None, 'head')
- grad_proj_out: float32 [2, 768, 1536], P(None, 'seq', 'head')
Inputs may be any that keep to these rules, and one draw needn't show every extreme that they name: `doc_lengths`: the 3 lengths sum to 4096, and the longest is exactly 2048.
All inputs are finite; a program needn't handle non-finite values.
Results may differ from a plain program's by a relative error of at most 0.0003.
Values sent between devices are 32-bit elements; how exact they have to be, the bound alone decides.
A program may use at most 192 MiB of HBM per device.

v0:
```python
from functools import partial
import jax
import jax.numpy as jnp
from jax import lax
from jax.sharding import PartitionSpec as P

STATE = 128
KERNEL = 4
BLOCK = 256
EPS = 1e-05
NEG_FILL = -1e30
EXACT = lax.Precision.HIGHEST
FAST = lax.Precision.HIGH


def passed_along(array, axis, by):
    count = lax.axis_size(axis)
    pairs = [(i, i + by) for i in range(count) if 0 <= i + by < count]
    return lax.ppermute(array, axis, pairs)


def product(spec, left, right, precision=FAST):
    return jnp.einsum(spec, left, right, precision=precision, preferred_element_type=jnp.float32)


def swish_act(values):
    return values * jax.nn.sigmoid(values)


def rms_scale(values):
    return lax.rsqrt(jnp.mean(values * values, axis=-1, keepdims=True) + EPS)


def segment_ids(doc_lengths, positions):
    ends = jnp.cumsum(doc_lengths)
    starts = ends - doc_lengths
    return jnp.sum((positions[:, None] >= starts[None, :]).astype(jnp.int32), axis=1) - 1


def widened(per_head, width):
    heads = per_head.shape[1]
    owner = jnp.arange(width) // (width // heads)
    spread = (jnp.arange(heads)[:, None] == owner[None, :]).astype(jnp.float32)
    return product("th,hc->tc", per_head, spread, EXACT)


def scaled_heads(state, factors):
    heads = factors.shape[0]
    return (state.reshape(heads, -1, state.shape[-1]) * factors[:, None, None]).reshape(state.shape)


def entering(pieces, decays, backward):
    count, mine = (lax.axis_size("seq"), lax.axis_index("seq"))
    order = jnp.arange(count)
    first, middle = (order[:, None], order[None, :])
    if backward:
        between = (middle > mine) & (middle < first)
        outside = order > mine
    else:
        between = (middle > first) & (middle < mine)
        outside = order < mine
    weights = jnp.prod(jnp.where(between[..., None], decays[None], 1.0), axis=1)
    weights = jnp.where(outside[:, None], weights, 0.0)
    heads = decays.shape[1]
    split = pieces.reshape(count, heads, -1, pieces.shape[-1])
    return jnp.sum(split * weights[:, :, None, None], axis=0).reshape(pieces.shape[1:])


def with_rows(rows, extra):
    width = rows.shape[1]
    more = -(-extra.shape[0] // (8 * width)) * 8
    return jnp.concatenate(
        [rows, jnp.pad(extra, (0, more * width - extra.shape[0])).reshape(more, width)], axis=0
    )


def front_fn(hidden, gain, weight_zx, weight_bd, inner_loc):
    normed = hidden * rms_scale(hidden) * gain[None, :]
    main = product("td,dc->tc", normed, weight_zx)
    side = product("td,dc->tc", normed, weight_bd)
    raw = jnp.concatenate([main[:, inner_loc:], side[:, : 2 * STATE]], axis=1)
    return (main[:, :inner_loc], raw, side[:, 2 * STATE :])


def conv_local(raw, prev_tail, kernel, bias, keeps):
    extended = jnp.concatenate([prev_tail, raw], axis=0)
    count = raw.shape[0]
    total = jnp.zeros_like(raw) + bias[None, :]
    for offset in range(KERNEL):
        total = total + kernel[offset][None, :] * extended[offset : offset + count] * keeps[offset]
    return swish_act(total)


def local_fn(values, dt_raw, dt_bias, a_log, skip_gain, bc, seg_now, seg_prev):
    count, width = values.shape
    heads = dt_raw.shape[1]
    rows = min(BLOCK, count)
    blocks = count // rows
    step_size = jax.nn.softplus(dt_raw + dt_bias)
    log_decay = -step_size * jnp.exp(a_log)
    order = jnp.arange(rows)
    lower = order[:, None] >= order[None, :]
    cum = product(
        "ts,bsh->bth", lower.astype(jnp.float32), log_decay.reshape(blocks, rows, heads), EXACT
    )
    cum_rows = cum.transpose(2, 0, 1)
    seg = seg_now.reshape(blocks, rows)
    before = jnp.concatenate([seg_prev[None], seg[:-1, -1]])
    allowed = lower[None] & (seg[:, :, None] == seg[:, None, :])
    spans = cum_rows[:, :, :, None] - cum_rows[:, :, None, :]
    decays = jnp.exp(jnp.where(allowed[None], spans, NEG_FILL))
    b_matrix = bc[:, :STATE].reshape(blocks, rows, STATE)
    c_matrix = bc[:, STATE:].reshape(blocks, rows, STATE)
    scores = decays * product("btn,bsn->bts", c_matrix, b_matrix)[None]
    stepped = values * widened(step_size, width)
    output = product(
        "hbts,bshp->bthp", scores, stepped.reshape(blocks, rows, heads, width // heads)
    ).reshape(count, width)
    output = output + jnp.repeat(skip_gain, width // heads)[None, :] * values
    last = cum[:, -1]
    enter = jnp.exp(cum) * (seg == before[:, None]).astype(jnp.float32)[..., None]
    keep_end = (seg == seg[:, -1:]).astype(jnp.float32)
    leave = jnp.exp(last[:, None] - cum) * keep_end[..., None]
    weighted = stepped * widened(leave.reshape(count, heads), width)
    states = product("bsc,bsn->bcn", weighted.reshape(blocks, rows, width), b_matrix)
    carries = jnp.exp(last) * (seg[:, -1] == before).astype(jnp.float32)[:, None]
    state, decay = (states[0], carries[0])
    for block in range(1, blocks):
        state = scaled_heads(state, carries[block]) + states[block]
        decay = decay * carries[block]
    return (output, enter.reshape(count, heads), states, carries, state, decay)


def mix_fn(output, enter, states, carries, state_in, bc):
    count, width = output.shape
    blocks = states.shape[0]
    entry = [state_in]
    for block in range(blocks - 1):
        entry.append(scaled_heads(entry[-1], carries[block]) + states[block])
    c_matrix = bc[:, STATE:].reshape(blocks, count // blocks, STATE)
    read = product("btn,bcn->btc", c_matrix, jnp.stack(entry)).reshape(count, width)
    return output + widened(enter, width) * read


def gate_fn(mixed, gate_in, gate_gain, proj_out_loc):
    gated = mixed * swish_act(gate_in)
    rows = product("tc,dc->td", gated * gate_gain[None, :], proj_out_loc)
    return (rows, jnp.sum(gated * gated, axis=1))


def body(
    hidden_in,
    grad_out,
    doc_lengths,
    norm_gain,
    proj_z,
    proj_x,
    proj_bc,
    proj_dt,
    conv_x_kernel,
    conv_x_bias,
    conv_bc_kernel,
    conv_bc_bias,
    dt_bias,
    a_log,
    skip_gain,
    gate_gain,
    proj_out,
):
    count, width = hidden_in.shape
    layers, rows_loc, inner_loc = proj_z.shape
    bc_loc = proj_bc.shape[2]
    heads = proj_dt.shape[2]
    inner = inner_loc * lax.axis_size("head")
    bc_all = 2 * STATE
    margin = KERNEL - 1
    positions = lax.axis_index("seq") * count + jnp.arange(-margin, count, dtype=jnp.int32)
    seg_ext = segment_ids(doc_lengths, positions)
    seg_now = seg_ext[margin:]
    seg_prev = seg_ext[margin - 1]
    keeps = [
        (seg_ext[offset : offset + count] == seg_now).astype(jnp.float32)[:, None]
        for offset in range(KERNEL)
    ]

    def over_seq(part):
        return lax.all_gather(part, "seq", axis=0, tiled=True)

    columns = lax.all_gather(
        jnp.concatenate([proj_bc, conv_bc_kernel, conv_bc_bias[:, None]], axis=1),
        "head",
        axis=2,
        tiled=True,
    )
    first = over_seq(
        jnp.concatenate(
            [proj_z[0], proj_x[0]]
            + [
                part
                for layer in range(layers)
                for part in (columns[layer, :rows_loc], proj_dt[layer])
            ],
            axis=1,
        )
    )
    rest = over_seq(
        jnp.concatenate(
            [proj_out[0]]
            + [
                part
                for layer in range(1, layers)
                for part in (proj_z[layer], proj_x[layer], proj_out[layer])
            ],
            axis=1,
        )
    )
    full_zx = [first[:, : 2 * inner_loc]]
    full_out = [rest[:, :inner_loc]]
    for layer in range(1, layers):
        at = (3 * layer - 2) * inner_loc
        full_zx.append(rest[:, at : at + 2 * inner_loc])
        full_out.append(rest[:, at + 2 * inner_loc : at + 3 * inner_loc])
    side = first[:, 2 * inner_loc :]
    side_width = bc_all + heads
    full_bd = [side[:, layer * side_width : (layer + 1) * side_width] for layer in range(layers)]
    hidden = hidden_in
    saved = []
    for layer in range(layers):
        front_out, pull_front = jax.vjp(
            partial(front_fn, inner_loc=inner_loc),
            hidden,
            norm_gain[layer],
            full_zx[layer],
            full_bd[layer],
        )
        gate_in, raw, dt_raw = front_out
        prev_tail = passed_along(raw[count - margin :], "seq", 1)
        kernel = jnp.concatenate(
            [conv_x_kernel[layer], columns[layer, rows_loc : rows_loc + KERNEL]], axis=1
        )
        bias = jnp.concatenate([conv_x_bias[layer], columns[layer, rows_loc + KERNEL]])
        conv_out, pull_conv = jax.vjp(
            partial(conv_local, keeps=keeps), raw, prev_tail, kernel, bias
        )
        values, bc = (conv_out[:, :inner_loc], conv_out[:, inner_loc:])
        local_out, pull_local = jax.vjp(
            partial(local_fn, seg_now=seg_now, seg_prev=seg_prev),
            values,
            dt_raw,
            dt_bias[layer],
            a_log[layer],
            skip_gain[layer],
            bc,
        )
        output, enter, states, carries, state_dev, decay_dev = local_out
        packed = jnp.concatenate(
            [state_dev, jnp.pad(decay_dev[None], ((0, 7), (0, STATE - heads)))], axis=0
        )
        pieces = lax.all_gather(packed, "seq")
        decays = pieces[:, inner_loc, :heads]
        state_in = entering(pieces[:, :inner_loc], decays, False)
        mixed, pull_mix = jax.vjp(mix_fn, output, enter, states, carries, state_in, bc)
        (rows, squares), pull_gate = jax.vjp(
            gate_fn, mixed, gate_in, gate_gain[layer], full_out[layer]
        )
        if layer < layers - 1:
            summed = lax.psum(with_rows(rows, squares), "head")
            total_sq = summed[count:].reshape(-1)[:count]
            scale = lax.rsqrt(total_sq / inner + EPS)
            sums = summed[:count]
            hidden = hidden + scale[:, None] * sums
            grad_scale = sums
        else:
            pair = lax.psum(jnp.stack([squares, jnp.sum(grad_out * rows, axis=1)]), "head")
            total_sq, grad_scale = (pair[0], pair[1])
            scale = lax.rsqrt(total_sq / inner + EPS)
            last_rows = scale[:, None] * rows
        saved.append(
            (
                pull_front,
                pull_conv,
                pull_local,
                pull_mix,
                pull_gate,
                scale,
                grad_scale,
                decays,
                state_in,
            )
        )
    grad_hidden = grad_out
    big, small = ([None] * layers for _ in range(2))
    own_bc = []
    for layer in reversed(range(layers)):
        (
            pull_front,
            pull_conv,
            pull_local,
            pull_mix,
            pull_gate,
            scale,
            grad_scale,
            decays,
            state_in,
        ) = saved[layer]
        if layer < layers - 1:
            grad_scale = jnp.sum(grad_hidden * grad_scale, axis=1)
        grad_squares = grad_scale * (-0.5 / inner) * scale * scale * scale
        grad_mixed, grad_gate_in, grad_ggain, grad_full_out = pull_gate(
            (scale[:, None] * grad_hidden, grad_squares)
        )
        grad_output, grad_enter, grad_states, grad_carries, grad_state_in, mix_bc = pull_mix(
            grad_mixed
        )
        grad_pieces = lax.all_gather(grad_state_in, "seq")
        if layer == layers - 1:
            grad_pieces, last_rows = lax.optimization_barrier((grad_pieces, last_rows))
            hidden_out = hidden + lax.psum(last_rows, "head")
        grad_state_end = entering(grad_pieces, decays, True)
        grad_decay = jnp.sum((grad_state_end * state_in).reshape(heads, -1), axis=1)
        grad_values, grad_dt_raw, grad_dbias, grad_alog, grad_skip, local_bc = pull_local(
            (grad_output, grad_enter, grad_states, grad_carries, grad_state_end, grad_decay)
        )
        grad_raw, grad_prev, grad_kernel, grad_cbias = pull_conv(
            jnp.concatenate([grad_values, mix_bc + local_bc], axis=1)
        )
        from_right = passed_along(grad_prev, "seq", -1)
        grad_raw = grad_raw + jnp.pad(from_right, ((count - margin, 0), (0, 0)))
        grad_part, grad_ngain, grad_zx, grad_bd = pull_front((grad_gate_in, grad_raw, grad_dt_raw))
        shared = jnp.concatenate(
            [grad_ngain, grad_kernel[:, inner_loc:].reshape(-1), grad_cbias[inner_loc:]]
        )
        if layer == layers - 1:
            grad_part, hidden_out = lax.optimization_barrier((grad_part, hidden_out))
        summed = lax.psum(with_rows(grad_part, shared), "head")
        grad_hidden = grad_hidden + summed[:count]
        shared = summed[count:].reshape(-1)[: shared.shape[0]]
        big[layer] = lax.psum_scatter(
            jnp.concatenate([grad_full_out, grad_zx, grad_bd], axis=1),
            "seq",
            scatter_dimension=0,
            tiled=True,
        )
        own_bc.append(
            lax.psum_scatter(
                big[layer][:, 3 * inner_loc : 3 * inner_loc + bc_all],
                "head",
                scatter_dimension=1,
                tiled=True,
            )
        )
        small[layer] = (
            grad_kernel[:, :inner_loc].reshape(-1),
            grad_cbias[:inner_loc],
            grad_ggain,
            grad_dbias,
            grad_alog,
            grad_skip,
            shared[:width],
            shared[width : width + KERNEL * bc_all],
            shared[width + KERNEL * bc_all :],
        )

    def laid_out(parts):
        sizes = [part.shape[0] for part in parts[0]]
        stacked = jnp.stack([jnp.concatenate(layer_parts) for layer_parts in parts])
        return (stacked, sizes)

    def taken(stacked, sizes):
        starts = [sum(sizes[:place]) for place in range(len(sizes))]
        return [stacked[:, start : start + size] for start, size in zip(starts, sizes)]

    stacked, sizes = laid_out(small)
    cxk, cxb, ggain, dbias, alog, skip, ngain, cbk, cbb = taken(lax.psum(stacked, "seq"), sizes)
    offset = lax.axis_index("head") * bc_loc
    cbk = lax.dynamic_slice_in_dim(cbk.reshape(layers, KERNEL, bc_all), offset, bc_loc, axis=2)
    cbb = lax.dynamic_slice_in_dim(cbb, offset, bc_loc, axis=1)
    return (
        hidden_out,
        grad_hidden,
        ngain,
        jnp.stack([part[:, inner_loc : 2 * inner_loc] for part in big]),
        jnp.stack([part[:, 2 * inner_loc : 3 * inner_loc] for part in big]),
        jnp.stack(own_bc[::-1]),
        jnp.stack([part[:, 3 * inner_loc + bc_all :] for part in big]),
        cxk.reshape(layers, KERNEL, inner_loc),
        cxb,
        cbk,
        cbb,
        dbias,
        alog,
        skip,
        ggain,
        jnp.stack([part[:, :inner_loc] for part in big]),
    )


def solution(mesh):
    in_specs = (
        P("seq", None),
        P("seq", None),
        P(),
        P(),
        P(None, "seq", "head"),
        P(None, "seq", "head"),
        P(None, "seq", "head"),
        P(None, "seq", "head"),
        P(None, None, "head"),
        P(None, "head"),
        P(None, None, "head"),
        P(None, "head"),
        P(None, "head"),
        P(None, "head"),
        P(None, "head"),
        P(None, "head"),
        P(None, "seq", "head"),
    )
    out_specs = (
        P("seq", None),
        P("seq", None),
        P(),
        P(None, "seq", "head"),
        P(None, "seq", "head"),
        P(None, "seq", "head"),
        P(None, "seq", "head"),
        P(None, None, "head"),
        P(None, "head"),
        P(None, None, "head"),
        P(None, "head"),
        P(None, "head"),
        P(None, "head"),
        P(None, "head"),
        P(None, "head"),
        P(None, "seq", "head"),
    )
    return jax.shard_map(body, mesh=mesh, in_specs=in_specs, out_specs=out_specs, check_vma=False)
```

profile of v0, /device:TPU:0, one launch (start us, length us, event | category | flops | bytes accessed | tf_op | source)
XLA Modules:
  0.0 822.2 jit_solution(18058968250045826087)
XLA Ops:
  10.9 15.7 %all_gather.29 = f32[2,101,256]{1,0,2:T(2,128)S(1)} all-gather(f32[2,101,64]{1,0,2:T(2,128)S(1)} %pad_maximum_fusion.19), channel_id=1, replica_groups=mesh['seq'=8,'head'=4] {'head'}, dimensions={2}, use_global_device_ids=true | all-gather | bytes 258560 | tf_op jit(solution)/shard_map/all_gather | solution.py:189
  34.5 4.4 slice_reduce_fusion.1
  42.0 25.6 %all-gather.9.cloned.1.call-done = f32[768,1292]{1,0:T(8,128)} async-done(((f32[96,1292]{1,0:T(8,128)}), f32[768,1292]{1,0:T(8,128)}) %all-gather.9.cloned.1.call-update) | async-done | bytes 3969040 | tf_op jit(solution)/shard_map/all_gather | solution.py:187
  102.4 3.1 fusion.70
  107.2 17.9 %all-gather.17.cloned.1.call-done = f32[3136,128]{1,0:T(8,128)} async-done(((f32[392,128]{1,0:T(8,128)}), f32[3136,128]{1,0:T(8,128)}) %all-gather.17.cloned.1.call-update) | async-done | bytes 1605648 | tf_op jit(solution)/shard_map/all_gather | solution.py:259
  133.5 4.0 multiply_reduce_fusion.23
  137.5 28.3 %all-gather.11.cloned.1.call-done = f32[768,1536]{1,0:T(8,128)} async-done(((f32[96,1536]{1,0:T(8,128)}), f32[768,1536]{1,0:T(8,128)}) %all-gather.11.cloned.1.call-update) | async-done | bytes 4718608 | tf_op jit(solution)/shard_map/all_gather | solution.py:187
  165.8 3.7 fusion.94
  173.0 67.9 %all-reduce.58.cloned.1.call-done = f32[520,768]{1,0:T(8,128)} async-done(((f32[520,768]{1,0:T(8,128)}), f32[520,768]{1,0:T(8,128)}) %all-reduce.58.cloned.1.call-update) | async-done | bytes 1597456 | tf_op jit(solution)/shard_map/psum | solution.py:267
  250.4 3.9 fusion.18
  268.3 3.3 fusion.316
  287.7 3.3 fusion.76
  292.6 15.9 %all-gather.19.cloned.1.call-done = f32[3136,128]{1,0:T(8,128)} async-done(((f32[392,128]{1,0:T(8,128)}), f32[3136,128]{1,0:T(8,128)}) %all-gather.19.cloned.1.call-update) | async-done | bytes 1605648 | tf_op jit(solution)/shard_map/all_gather | solution.py:259
  324.7 3.9 multiply_reduce_fusion.22
  328.6 4.9 multiply_reduce_fusion.7
  334.2 12.4 %psum.43 = f32[2,512]{1,0:T(2,128)} all-reduce(f32[2,512]{1,0:T(2,128)} %pad_maximum_fusion.25), channel_id=1, replica_groups=mesh['seq'=8,'head'=4] {'head'}, use_global_device_ids=true, to_apply=%region_12.14 | all-reduce | flops 1024 | bytes 8192 | tf_op jit(solution)/shard_map/psum | solution.py:274
  347.4 3.2 fusion.62
  350.6 3.4 multiply_reduce_fusion.18
  374.9 5.3 fusion.25
  420.7 4.9 fusion.89
  425.6 35.7 %all-reduce.60.cloned.1.call-done = f32[512,768]{1,0:T(8,128)} async-done(((f32[512,768]{1,0:T(8,128)}), f32[512,768]{1,0:T(8,128)}) %all-reduce.60.cloned.1.call-update) | async-done | bytes 1572880 | tf_op jit(solution)/shard_map/psum | solution.py:318
  461.3 8.4 %multiply_reduce_fusion.4 = (f32[768]{0:T(1024)S(1)}, f32[512]{0:T(512)S(1)}, f32[512,768]{1,0:T(8,128)}, f32[512,768]{1,0:T(8,128)S(1)}) fusion(f32[512,768]{1,0:T(8,128)S(1)} %get-tuple-element.205, f32[512]{0:T(512)S(1)} %fusion.283, f32[768]{0:T(1024)S(1)} %copy-done.112, f32[512,768]{1,0:T(8,128)} %all-reduce.60.cloned.1.call-done, ...), kind=kOutput, calls=%fused_computation.58 | convolution fusion | flops 1815476992 | bytes 11806720 | tf_op jit(solution)/shard_map/transpose(jvp(td,dc->tc))/dot_general | solution.py:23
  474.2 69.0 %all-reduce.62.cloned.1.call-done = f32[520,768]{1,0:T(8,128)} async-done(((f32[520,768]{1,0:T(8,128)}), f32[520,768]{1,0:T(8,128)}) %all-reduce.62.cloned.1.call-update) | async-done | bytes 1597456 | tf_op jit(solution)/shard_map/psum | solution.py:335
  569.6 5.9 copy.495
  581.0 5.3 fusion.27
  624.5 4.4 multiply_reduce_fusion.1
  640.6 6.0 copy.493
  654.0 62.4 %all-reduce.64.cloned.1.call-done = f32[520,768]{1,0:T(8,128)} async-done(((f32[520,768]{1,0:T(8,128)}), f32[520,768]{1,0:T(8,128)}) %all-reduce.64.cloned.1.call-update) | async-done | bytes 1597456 | tf_op jit(solution)/shard_map/psum | solution.py:335
  717.2 23.5 %psum.47 = f32[2,4370]{1,0:T(2,128)S(1)} all-reduce(f32[2,4370]{1,0:T(2,128)S(1)} %pad_maximum_fusion.21), channel_id=1, replica_groups=mesh['seq'=8,'head'=4] {'seq'}, use_global_device_ids=true, to_apply=%region_65.67 | all-reduce | flops 8740 | bytes 69920 | tf_op jit(solution)/shard_map/psum | solution.py:374
  747.5 25.1 %reduce-scatter.13.cloned.1.call-done = f32[96,1414]{1,0:T(8,128)} async-done(((f32[768,1414]{1,0:T(8,128)}), f32[96,1414]{1,0:T(8,128)}) %reduce-scatter.13.cloned.1.call-update) | async-done | bytes 542992
  780.0 14.4 %reduce-scatter.11.cloned.1.call-done = f32[96,64]{0,1:T(8,128)} async-done(((f32[96,256]{0,1:T(8,128)}), f32[96,64]{0,1:T(8,128)}) %reduce-scatter.11.cloned.1.call-update) | async-done | bytes 24592 | tf_op jit(solution)/shard_map/reduce_scatter | solution.py:345
  794.3 19.8 %reduce-scatter.9.cloned.1.call-done = f32[96,64]{0,1:T(8,128)} async-done(((f32[96,256]{0,1:T(8,128)}), f32[96,64]{0,1:T(8,128)}) %reduce-scatter.9.cloned.1.call-update) | async-done | bytes 24592 | tf_op jit(solution)/shard_map/reduce_scatter | solution.py:345
  (878 shorter events, 290.1 us)
Async XLA Ops:
  7.2 60.3 %all-gather.9.cloned.1.call-start = ((), (), s32[]{:S(2)}) async-start(), calls=%async_computation.4 | async-start | bytes 4866048 | tf_op jit(solution)/shard_map/all_gather | solution.py:187
  28.7 96.4 %all-gather.17.cloned.1.call-start = ((), (), s32[]{:S(2)}) async-start(), calls=%async_computation.14 | async-start | bytes 1806336 | tf_op jit(solution)/shard_map/all_gather | solution.py:259
  32.3 48.5 %copy-start.143 = (f32[640]{0:T(1024)}, f32[640]{0:T(1024)S(1)}, u32[]{:S(2)}) copy-start(f32[640]{0:T(1024)S(1)} %get-tuple-element.174) | copy-start | bytes 7684
  32.3 48.5 %copy-start.145 = (f32[640]{0:T(1024)}, f32[640]{0:T(1024)S(1)}, u32[]{:S(2)}) copy-start(f32[640]{0:T(1024)S(1)} %get-tuple-element.175) | copy-start | bytes 7684
  32.3 48.5 %copy-start.147 = (f32[640]{0:T(1024)}, f32[640]{0:T(1024)S(1)}, u32[]{:S(2)}) copy-start(f32[640]{0:T(1024)S(1)} %get-tuple-element.177) | copy-start | bytes 7684
  32.3 48.5 %copy-start.149 = (f32[640]{0:T(1024)}, f32[640]{0:T(1024)S(1)}, u32[]{:S(2)}) copy-start(f32[640]{0:T(1024)S(1)} %get-tuple-element.176) | copy-start | bytes 7684
  33.7 37.2 %copy-start.106 = (s32[384]{0:T(512)}, s32[384]{0:T(512)S(1)}, u32[]{:S(2)}) copy-start(s32[384]{0:T(512)S(1)} %add_select_fusion) | copy-start | bytes 4612
  40.4 37.9 %copy-start.201 = (f32[2]{0:T(128)}, f32[2]{0:T(128)S(1)}, u32[]{:S(2)}) copy-start(f32[2]{0:T(128)S(1)} %fusion.284) | copy-start | bytes 28
  41.9 36.4 %copy-start.195 = (f32[2,256]{1,0:T(2,128)}, f32[2,256]{1,0:T(2,128)S(1)}, u32[]{:S(2)}) copy-start(f32[2,256]{1,0:T(2,128)S(1)} %get-tuple-element.272) | copy-start | bytes 6148
  42.0 38.9 %copy-start.121 = (f32[512]{0:T(512)}, f32[512]{0:T(512)S(1)}, u32[]{:S(2)}) copy-start(f32[512]{0:T(512)S(1)} %get-tuple-element.268) | copy-start | bytes 6148
  42.0 38.9 %copy-start.123 = (f32[512]{0:T(512)}, f32[512]{0:T(512)S(1)}, u32[]{:S(2)}) copy-start(f32[512]{0:T(512)S(1)} %get-tuple-element.269) | copy-start | bytes 6148
  42.0 38.9 %copy-start.126 = (f32[512]{0:T(512)}, f32[512]{0:T(512)S(1)}, u32[]{:S(2)}) copy-start(f32[512]{0:T(512)S(1)} %get-tuple-element.270) | copy-start | bytes 6148
  76.1 4.2 collective-permute-start
  94.1 71.7 %all-gather.11.cloned.1.call-start = ((), (), s32[]{:S(2)}) async-start(), calls=%async_computation.5 | async-start | bytes 5308416 | tf_op jit(solution)/shard_map/all_gather | solution.py:187
  97.2 143.7 %all-reduce.58.cloned.1.call-start = ((), (), s32[]{:S(2)}) async-start(), calls=%async_computation.6 | async-start | bytes 3194880 | tf_op jit(solution)/shard_map/psum | solution.py:267
  98.8 67.0 %copy-start.160 = (f32[384]{0:T(512)}, f32[384]{0:T(512)S(1)}, u32[]{:S(2)}) copy-start(f32[384]{0:T(512)S(1)} %get-tuple-element.185) | copy-start | bytes 4612
  99.6 283.5 %copy-start.113 = (pred[2,256,256]{2,1,0:T(8,128)(4,1)}, pred[2,256,256]{2,1,0:T(8,128)(4,1)S(1)}, u32[]{:S(2)}) copy-start(pred[2,256,256]{2,1,0:T(8,128)(4,1)S(1)} %compare_and_fusion) | copy-start | bytes 393220
  170.8 137.6 %all-gather.19.cloned.1.call-start = ((), (), s32[]{:S(2)}) async-start(), calls=%async_computation.15 | async-start | bytes 1806336 | tf_op jit(solution)/shard_map/all_gather | solution.py:259
  256.6 3.4 collective-permute-start.1
  278.2 111.5 %all-gather.13.cloned.1.call-start = ((), (), s32[]{:S(2)}) async-start(), calls=%async_computation.7 | async-start | bytes 1769472 | tf_op jit(solution)/shard_map/all_gather | solution.py:315
  362.5 98.8 %all-reduce.60.cloned.1.call-start = ((), (), s32[]{:S(2)}) async-start(), calls=%async_computation.8 | async-start | bytes 3145728 | tf_op jit(solution)/shard_map/psum | solution.py:318
  394.9 148.3 %all-reduce.62.cloned.1.call-start = ((), (), s32[]{:S(2)}) async-start(), calls=%async_computation.9 | async-start | bytes 3194880 | tf_op jit(solution)/shard_map/psum | solution.py:335
  413.5 5.6 collective-permute-start.2
  474.0 72.7 %copy-start.167 = (f32[512]{0:T(512)S(1)}, f32[512]{0:T(512)}, u32[]{:S(2)}) copy-start(f32[512]{0:T(512)} %copy-done.166) | copy-start | bytes 6148
  474.0 120.1 %all-gather.15.cloned.1.call-start = ((), (), s32[]{:S(2)}) async-start(), calls=%async_computation.10 | async-start | bytes 1769472 | tf_op jit(solution)/shard_map/all_gather | solution.py:315
  559.6 90.3 %reduce-scatter.15.cloned.1.call-start = ((), (), s32[]{:S(2)}) async-start(), calls=%async_computation.17 | async-start | bytes 5308416
  575.6 140.8 %all-reduce.64.cloned.1.call-start = ((), (), s32[]{:S(2)}) async-start(), calls=%async_computation.11 | async-start | bytes 3194880 | tf_op jit(solution)/shard_map/psum | solution.py:335
  616.9 4.6 collective-permute-start.3
  630.5 142.1 %reduce-scatter.13.cloned.1.call-start = ((), (), s32[]{:S(2)}) async-start(), calls=%async_computation.16 | async-start | bytes 5308416
  646.7 70.4 %copy-start.218 = (f32[384]{0:T(512)S(1)}, f32[384]{0:T(512)}, u32[]{:S(2)}) copy-start(f32[384]{0:T(512)} %get-tuple-element.215) | copy-start | bytes 4612
  646.7 147.6 %reduce-scatter.11.cloned.1.call-start = ((), (), s32[]{:S(2)}) async-start(), calls=%async_computation.13 | async-start | bytes 163840 | tf_op jit(solution)/shard_map/reduce_scatter | solution.py:345
  653.9 160.2 %reduce-scatter.9.cloned.1.call-start = ((), (), s32[]{:S(2)}) async-start(), calls=%async_computation.12 | async-start | bytes 163840 | tf_op jit(solution)/shard_map/reduce_scatter | solution.py:345
  (239 other events, 1052.9 us)
Sparse Core Ops, SparseCore 0:
  28.8 38.6 all-gather.8
  94.3 30.8 all-gather.16
  127.0 38.7 all-gather.10
  170.9 69.9 all-reduce.57
  278.4 30.0 all-gather.18
  362.6 22.7 all-gather.12
  395.1 66.2 all-reduce.59
  474.1 69.0 all-reduce.61
  559.7 24.6 all-gather.14
  587.7 56.1 reduce-scatter.14
  646.4 69.9 all-reduce.63
  719.6 52.8 reduce-scatter.12
  774.8 19.4 reduce-scatter.10
  796.4 17.6 reduce-scatter.8
where the time goes:
time: 834 us; the launch traced here: 822 us
  waiting for transfers between devices  382 us (46%)
  matrix products  136 us (16%)
  local copies, waits for them, and re-layouts  131 us (16%)
  other arithmetic  94.6 us (11%)
  blocking collectives  51.5 us (6%)
  between operations  17.4 us (2%)
  starting transfers between devices  9.89 us (1%)
    dot_general x58, matrix products, product(): jnp.einsum(spec, left, right, precision=precision, preferred_element_type...  136 us
    psum x2, waiting for transfers between devices, body(): summed = lax.psum(with_rows(grad_part, shared), 'head')  131 us
    psum x1, waiting for transfers between devices, body(): summed = lax.psum(with_rows(rows, squares), 'head')  67.9 us
    all_gather x2, waiting for transfers between devices, over_seq(): return lax.all_gather(part, 'seq', axis=0, tiled=True)  53.9 us
    unnamed x524, local copies, waits for them, and re-layouts  42.1 us
    psum x1, waiting for transfers between devices, body(): hidden_out = hidden + lax.psum(last_rows, 'head')  35.7 us
    reduce_scatter x2, waiting for transfers between devices, body(): lax.psum_scatter(big[layer][:, 3 * inner_loc:3 * inner_loc + bc_all], 'he...  34.1 us
    all_gather x2, waiting for transfers between devices, body(): pieces = lax.all_gather(packed, 'seq')  33.8 us
  transfers between devices with their start and end apart: 18, of which 11 were waited for; matrix products, arithmetic and copies ran while one was open for 25% of the time, Pallas kernels for 0%

commit v1 on v0

--- a/solution.py
+++ b/solution.py
@@ -332,7 +332,7 @@
         )
         if layer == layers - 1:
             grad_part, hidden_out = lax.optimization_barrier((grad_part, hidden_out))
-        summed = lax.psum(with_rows(grad_part, shared), "head")
+        summed = jnp.sum(lax.all_gather(with_rows(grad_part, shared), "head"), axis=0)
         grad_hidden = grad_hidden + summed[:count]
         shared = summed[count:].reshape(-1)[: shared.shape[0]]
         big[layer] = lax.psum_scatter(

time: 834 us -> 964 us (1.16)
  waiting for transfers between devices: 382 us -> 498 us
  other arithmetic: 94.6 us -> 106 us
    all_gather x0 -> x2, waiting for transfers between devices: none -> 231 us  [body(): lax.all_gather(with_rows(grad_part, shared), 'head')]
    psum x2 -> x0, waiting for transfers between devices: 131 us -> none  [body(): summed = lax.psum(with_rows(grad_part, shared), 'head')]
    unnamed x16, waiting for transfers between devices: 25.4 us -> 47.6 us
    unnamed x524 -> x534, local copies, waits for them, and re-layouts: 42.1 us -> 43.1 us
  transfers between devices with their start and end apart: 18 -> 18, of which waited for: 11 -> 12; matrix products, arithmetic and copies ran while one was open for 25% -> 22% of each run, Pallas kernels for 0% -> 0%
where the time goes in v1:
time: 964 us; the launch traced here: 952 us
  waiting for transfers between devices  498 us (52%)
  matrix products  138 us (14%)
  local copies, waits for them, and re-layouts  129 us (13%)
  other arithmetic  106 us (11%)
  blocking collectives  52.5 us (5%)
  between operations  17.5 us (2%)
  starting transfers between devices  10.3 us (1%)
    all_gather x2, waiting for transfers between devices, body(): lax.all_gather(with_rows(grad_part, shared), 'head')  231 us
    dot_general x58, matrix products, product(): jnp.einsum(spec, left, right, precision=precision, preferred_element_type...  138 us
    psum x1, waiting for transfers between devices, body(): summed = lax.psum(with_rows(rows, squares), 'head')  67.9 us
    all_gather x2, waiting for transfers between devices, over_seq(): return lax.all_gather(part, 'seq', axis=0, tiled=True)  53.9 us
    unnamed x16, waiting for transfers between devices  47.6 us
    unnamed x534, local copies, waits for them, and re-layouts  43.1 us
    psum x1, waiting for transfers between devices, body(): hidden_out = hidden + lax.psum(last_rows, 'head')  36 us
    all_gather x2, waiting for transfers between devices, body(): pieces = lax.all_gather(packed, 'seq')  33.5 us
  transfers between devices with their start and end apart: 18, of which 12 were waited for; matrix products, arithmetic and copies ran while one was open for 22% of the time, Pallas kernels for 0%

profile of v1, /device:TPU:0, one launch (start us, length us, event | category | flops | bytes accessed | tf_op | source)
XLA Modules:
  0.0 951.6 jit_solution(13723462105524682835)
XLA Ops:
  10.9 15.7 %all_gather.41 = f32[2,101,256]{1,0,2:T(2,128)S(1)} all-gather(f32[2,101,64]{1,0,2:T(2,128)S(1)} %pad_maximum_fusion.19), channel_id=1, replica_groups=mesh['seq'=8,'head'=4] {'head'}, dimensions={2}, use_global_device_ids=true | all-gather | bytes 258560 | tf_op jit(solution)/shard_map/all_gather | solution.py:189
  34.5 4.4 slice_reduce_fusion.1
  42.0 25.5 %all-gather.13.cloned.1.call-done = f32[768,1292]{1,0:T(8,128)} async-done(((f32[96,1292]{1,0:T(8,128)}), f32[768,1292]{1,0:T(8,128)}) %all-gather.13.cloned.1.call-update) | async-done | bytes 3969040 | tf_op jit(solution)/shard_map/all_gather | solution.py:187
  107.6 17.7 %all-gather.21.cloned.1.call-done = f32[3136,128]{1,0:T(8,128)} async-done(((f32[392,128]{1,0:T(8,128)}), f32[3136,128]{1,0:T(8,128)}) %all-gather.21.cloned.1.call-update) | async-done | bytes 1605648 | tf_op jit(solution)/shard_map/all_gather | solution.py:259
  133.6 4.0 multiply_reduce_fusion.23
  137.6 28.4 %all-gather.15.cloned.1.call-done = f32[768,1536]{1,0:T(8,128)} async-done(((f32[96,1536]{1,0:T(8,128)}), f32[768,1536]{1,0:T(8,128)}) %all-gather.15.cloned.1.call-update) | async-done | bytes 4718608 | tf_op jit(solution)/shard_map/all_gather | solution.py:187
  165.9 3.7 fusion.94
  173.1 67.9 %all-reduce.56.cloned.1.call-done = f32[520,768]{1,0:T(8,128)} async-done(((f32[520,768]{1,0:T(8,128)}), f32[520,768]{1,0:T(8,128)}) %all-reduce.56.cloned.1.call-update) | async-done | bytes 1597456 | tf_op jit(solution)/shard_map/psum | solution.py:267
  250.5 3.9 fusion.18
  292.7 15.8 %all-gather.23.cloned.1.call-done = f32[3136,128]{1,0:T(8,128)} async-done(((f32[392,128]{1,0:T(8,128)}), f32[3136,128]{1,0:T(8,128)}) %all-gather.23.cloned.1.call-update) | async-done | bytes 1605648 | tf_op jit(solution)/shard_map/all_gather | solution.py:259
  324.9 3.9 multiply_reduce_fusion.22
  328.8 4.9 multiply_reduce_fusion.7
  334.3 12.4 %psum.29 = f32[2,512]{1,0:T(2,128)} all-reduce(f32[2,512]{1,0:T(2,128)} %pad_maximum_fusion.25), channel_id=1, replica_groups=mesh['seq'=8,'head'=4] {'head'}, use_global_device_ids=true, to_apply=%region_12.14 | all-reduce | flops 1024 | bytes 8192 | tf_op jit(solution)/shard_map/psum | solution.py:274
  350.7 3.4 multiply_reduce_fusion.18
  375.2 5.3 fusion.25
  420.8 4.9 fusion.89
  425.7 36.0 %all-reduce.58.cloned.1.call-done = f32[512,768]{1,0:T(8,128)} async-done(((f32[512,768]{1,0:T(8,128)}), f32[512,768]{1,0:T(8,128)}) %all-reduce.58.cloned.1.call-update) | async-done | bytes 1572880 | tf_op jit(solution)/shard_map/psum | solution.py:318
  461.7 8.3 multiply_reduce_fusion.4
  474.5 116.0 %all-gather.25.cloned.1.call-done = f32[2080,768]{1,0:T(8,128)} async-done(((f32[520,768]{1,0:T(8,128)}), f32[2080,768]{1,0:T(8,128)}) %all-gather.25.cloned.1.call-update) | async-done | bytes 6389776 | tf_op jit(solution)/shard_map/all_gather | solution.py:335
  590.5 4.6 reduce_sum.580
  621.5 5.9 copy.495
  633.0 5.2 fusion.27
  683.9 5.9 copy.493
  689.9 3.5 reduce-scatter.15.cloned.1.call-done
  695.5 3.7 fusion.96
  699.2 6.0 multiply_reduce_fusion.1
  706.8 43.9 %reduce-scatter.13.cloned.1.call-done = f32[96,1414]{1,0:T(8,128)} async-done(((f32[768,1414]{1,0:T(8,128)}), f32[96,1414]{1,0:T(8,128)}) %reduce-scatter.13.cloned.1.call-update) | async-done | bytes 542992
  763.9 8.4 reduce-scatter.11.cloned.1.call-done
  772.3 19.9 %reduce-scatter.9.cloned.1.call-done = f32[96,64]{0,1:T(8,128)} async-done(((f32[96,256]{0,1:T(8,128)}), f32[96,64]{0,1:T(8,128)}) %reduce-scatter.9.cloned.1.call-update) | async-done | bytes 24592 | tf_op jit(solution)/shard_map/reduce_scatter | solution.py:345
  793.6 115.1 %all-gather.27.cloned.1.call-done = f32[2080,768]{1,0:T(8,128)} async-done(((f32[520,768]{1,0:T(8,128)}), f32[2080,768]{1,0:T(8,128)}) %all-gather.27.cloned.1.call-update) | async-done | bytes 6389776 | tf_op jit(solution)/shard_map/all_gather | solution.py:335
  908.8 4.7 reduce_sum.695
  916.3 24.5 %psum.31 = f32[2,4370]{1,0:T(2,128)S(1)} all-reduce(f32[2,4370]{1,0:T(2,128)S(1)} %pad_maximum_fusion.21), channel_id=1, replica_groups=mesh['seq'=8,'head'=4] {'seq'}, use_global_device_ids=true, to_apply=%region_65.67 | all-reduce | flops 8740 | bytes 69920 | tf_op jit(solution)/shard_map/psum | solution.py:374
  (892 shorter events, 300.8 us)
Async XLA Ops:
  7.2 60.3 %all-gather.13.cloned.1.call-start = ((), (), s32[]{:S(2)}) async-start(), calls=%async_computation.4 | async-start | bytes 4866048 | tf_op jit(solution)/shard_map/all_gather | solution.py:187
  28.7 96.5 %all-gather.21.cloned.1.call-start = ((), (), s32[]{:S(2)}) async-start(), calls=%async_computation.12 | async-start | bytes 1806336 | tf_op jit(solution)/shard_map/all_gather | solution.py:259
  32.3 48.5 %copy-start.150 = (f32[640]{0:T(1024)}, f32[640]{0:T(1024)S(1)}, u32[]{:S(2)}) copy-start(f32[640]{0:T(1024)S(1)} %get-tuple-element.174) | copy-start | bytes 7684
  32.3 48.5 %copy-start.152 = (f32[640]{0:T(1024)}, f32[640]{0:T(1024)S(1)}, u32[]{:S(2)}) copy-start(f32[640]{0:T(1024)S(1)} %get-tuple-element.175) | copy-start | bytes 7684
  32.3 48.5 %copy-start.154 = (f32[640]{0:T(1024)}, f32[640]{0:T(1024)S(1)}, u32[]{:S(2)}) copy-start(f32[640]{0:T(1024)S(1)} %get-tuple-element.177) | copy-start | bytes 7684
  32.3 48.5 %copy-start.156 = (f32[640]{0:T(1024)}, f32[640]{0:T(1024)S(1)}, u32[]{:S(2)}) copy-start(f32[640]{0:T(1024)S(1)} %get-tuple-element.176) | copy-start | bytes 7684
  33.7 37.2 %copy-start.113 = (s32[384]{0:T(512)}, s32[384]{0:T(512)S(1)}, u32[]{:S(2)}) copy-start(s32[384]{0:T(512)S(1)} %add_select_fusion) | copy-start | bytes 4612
  40.4 37.9 %copy-start.208 = (f32[2]{0:T(128)}, f32[2]{0:T(128)S(1)}, u32[]{:S(2)}) copy-start(f32[2]{0:T(128)S(1)} %fusion.284) | copy-start | bytes 28
  41.9 36.4 %copy-start.140 = (f32[2,256]{1,0:T(2,128)}, f32[2,256]{1,0:T(2,128)S(1)}, u32[]{:S(2)}) copy-start(f32[2,256]{1,0:T(2,128)S(1)} %get-tuple-element.271) | copy-start | bytes 6148
  41.9 36.4 %copy-start.202 = (f32[2,256]{1,0:T(2,128)}, f32[2,256]{1,0:T(2,128)S(1)}, u32[]{:S(2)}) copy-start(f32[2,256]{1,0:T(2,128)S(1)} %get-tuple-element.272) | copy-start | bytes 6148
  42.0 38.9 %copy-start.128 = (f32[512]{0:T(512)}, f32[512]{0:T(512)S(1)}, u32[]{:S(2)}) copy-start(f32[512]{0:T(512)S(1)} %get-tuple-element.268) | copy-start | bytes 6148
  42.0 38.9 %copy-start.130 = (f32[512]{0:T(512)}, f32[512]{0:T(512)S(1)}, u32[]{:S(2)}) copy-start(f32[512]{0:T(512)S(1)} %get-tuple-element.269) | copy-start | bytes 6148
  42.0 38.9 %copy-start.133 = (f32[512]{0:T(512)}, f32[512]{0:T(512)S(1)}, u32[]{:S(2)}) copy-start(f32[512]{0:T(512)S(1)} %get-tuple-element.270) | copy-start | bytes 6148
  76.1 4.2 collective-permute-start
  94.3 71.7 %all-gather.15.cloned.1.call-start = ((), (), s32[]{:S(2)}) async-start(), calls=%async_computation.5 | async-start | bytes 5308416 | tf_op jit(solution)/shard_map/all_gather | solution.py:187
  97.2 143.8 %all-reduce.56.cloned.1.call-start = ((), (), s32[]{:S(2)}) async-start(), calls=%async_computation.6 | async-start | bytes 3194880 | tf_op jit(solution)/shard_map/psum | solution.py:267
  99.1 66.8 %copy-start.167 = (f32[384]{0:T(512)}, f32[384]{0:T(512)S(1)}, u32[]{:S(2)}) copy-start(f32[384]{0:T(512)S(1)} %get-tuple-element.185) | copy-start | bytes 4612
  99.9 283.5 %copy-start.120 = (pred[2,256,256]{2,1,0:T(8,128)(4,1)}, pred[2,256,256]{2,1,0:T(8,128)(4,1)S(1)}, u32[]{:S(2)}) copy-start(pred[2,256,256]{2,1,0:T(8,128)(4,1)S(1)} %compare_and_fusion) | copy-start | bytes 393220
  170.9 137.6 %all-gather.23.cloned.1.call-start = ((), (), s32[]{:S(2)}) async-start(), calls=%async_computation.13 | async-start | bytes 1806336 | tf_op jit(solution)/shard_map/all_gather | solution.py:259
  256.8 3.3 collective-permute-start.1
  278.3 111.8 %all-gather.17.cloned.1.call-start = ((), (), s32[]{:S(2)}) async-start(), calls=%async_computation.7 | async-start | bytes 1769472 | tf_op jit(solution)/shard_map/all_gather | solution.py:315
  362.6 99.1 %all-reduce.58.cloned.1.call-start = ((), (), s32[]{:S(2)}) async-start(), calls=%async_computation.8 | async-start | bytes 3145728 | tf_op jit(solution)/shard_map/psum | solution.py:318
  395.2 195.3 %all-gather.25.cloned.1.call-start = ((), (), s32[]{:S(2)}) async-start(), calls=%async_computation.14 | async-start | bytes 7987200 | tf_op jit(solution)/shard_map/all_gather | solution.py:335
  413.8 5.3 collective-permute-start.2
  474.3 173.2 %all-gather.19.cloned.1.call-start = ((), (), s32[]{:S(2)}) async-start(), calls=%async_computation.9 | async-start | bytes 1769472 | tf_op jit(solution)/shard_map/all_gather | solution.py:315
  611.4 82.0 %reduce-scatter.15.cloned.1.call-start = ((), (), s32[]{:S(2)}) async-start(), calls=%async_computation.17 | async-start | bytes 5308416
  627.5 123.2 %reduce-scatter.13.cloned.1.call-start = ((), (), s32[]{:S(2)}) async-start(), calls=%async_computation.16 | async-start | bytes 5308416
  672.1 4.7 collective-permute-start.3
  689.9 82.4 %reduce-scatter.11.cloned.1.call-start = ((), (), s32[]{:S(2)}) async-start(), calls=%async_computation.11 | async-start | bytes 163840 | tf_op jit(solution)/shard_map/reduce_scatter | solution.py:345
  695.1 97.1 %reduce-scatter.9.cloned.1.call-start = ((), (), s32[]{:S(2)}) async-start(), calls=%async_computation.10 | async-start | bytes 163840 | tf_op jit(solution)/shard_map/reduce_scatter | solution.py:345
  705.3 47.1 %slice-start.5 = ((f32[1,640]{1,0:T(1,128)}), f32[1,256]{1,0:T(1,128)S(1)}, s32[]{:S(2)}) async-start(f32[1,640]{1,0:T(1,128)} %copy-done.229), calls=%async_computation.23 | async-start | bytes 2048 | tf_op jit(solution)/shard_map/slice | solution.py:331
  752.3 156.4 %all-gather.27.cloned.1.call-start = ((), (), s32[]{:S(2)}) async-start(), calls=%async_computation.15 | async-start | bytes 7987200 | tf_op jit(solution)/shard_map/all_gather | solution.py:335
  (247 other events, 1032.0 us)
Sparse Core Ops, SparseCore 0:
  28.8 38.6 all-gather.12
  94.4 30.8 all-gather.20
  127.1 38.7 all-gather.14
  171.0 69.9 all-reduce.55
  278.4 30.0 all-gather.22
  362.7 22.7 all-gather.16
  395.4 66.2 all-reduce.57
  474.4 116.0 all-gather.24
  611.6 23.7 all-gather.18
  638.6 54.7 reduce-scatter.14
  696.9 53.7 reduce-scatter.12
  752.8 19.4 reduce-scatter.10
  774.5 17.6 reduce-scatter.8
  793.6 115.0 all-gather.26
